TPU v7x, 32 devices: a whole 2x2x4 slice. The times are simulated.
32 devices in a mesh: groups: 2 (over x), frames: 16 (over z, y, core).
Axes of the slice: x: 2, y: 2, z: 4, core: 2. Of those that a mesh axis runs over, the one named last changes fastest.
Arguments:
- latents: bfloat16 [4, 64, 128, 320], P('groups', 'frames'), parts along dimension 0, may hold values from -6 to 6
- in_weight: bfloat16 [3, 3, 320, 320], replicated, may hold values from -0.109375 to 0.109375
- time_weight: bfloat16 [3, 320, 320], replicated, may hold values from -0.1875 to 0.1875
- mid_weight: bfloat16 [3, 3, 320, 640], replicated, may hold values from -0.109375 to 0.109375
- up_weight: bfloat16 [3, 3, 960, 320], replicated, may hold values from -0.0625 to 0.0625
Outputs:
- mixed: bfloat16 [4, 64, 128, 320], P('groups', 'frames'), parts along dimension 0
There are 2 independent parts, one for each index of `groups`. A program takes and returns all parts, laid end to end along the dimension named above; an argument that names none is the same for every part. Nothing has to cross between parts.
All inputs are finite; a program needn't handle non-finite values.
Results may differ from a plain program's by a relative error of at most 0.0045.
Values may be sent and summed in bfloat16 or wider, within the bound.
A program may use at most 64 MiB of HBM per device.

v0:
```python
import functools

import jax
import jax.numpy as jnp
from jax import lax
from jax.experimental import pallas as pl
from jax.experimental.pallas import tpu as pltpu
from jax.sharding import PartitionSpec as P

FRAMES = 4
MESH = pl.DeviceIdType.MESH
F32 = jnp.float32
BF16 = jnp.bfloat16


def mm(a, b):
    return jnp.dot(a, b, preferred_element_type=F32)


def later(v):
    at = lax.broadcasted_iota(jnp.int32, v.shape, 0)
    return jnp.where(at == 0, 0.0, pltpu.roll(v, 1, 0))


def sooner(v):
    at = lax.broadcasted_iota(jnp.int32, v.shape, 0)
    return jnp.where(at == v.shape[0] - 1, 0.0, pltpu.roll(v, v.shape[0] - 1, 0))


def silu(v):
    return v / (1.0 + jnp.exp(-v))


def kernel(
    count, x_hbm, in_hbm, time_hbm, mid_hbm, up_hbm, out_hbm,
    x3, s3, m3, win, wtime, wmid, wup, wskip, wpool, raw, raw_got, base, mine, got, edge,
    edge_got, middle, mid_acc, acc, out_v, passing,
    w_sem, x_sem, o_sem, h_send, h_recv, t_send, t_recv, e_send, e_recv, r_send, r_recv,
):
    clips, rows, c, columns = x_hbm.shape
    half, double = columns // 2, 2 * c
    pooled_rows = rows // 2
    bands = count // FRAMES
    idx = lax.axis_index("frames")
    placed = lax.rem(idx + bands // 2, count)
    band = lax.rem(placed, bands)
    frame = placed // bands
    has = {
        "up": band > 0,
        "down": band < bands - 1,
        "prev": frame > 0,
        "next": frame < FRAMES - 1,
    }
    who = {
        "up": lax.rem(idx + count - 1, count),
        "down": lax.rem(idx + 1, count),
        "prev": lax.rem(idx + count - bands, count),
        "next": lax.rem(idx + bands, count),
    }

    reach = bands // 2
    detour = bands == 4
    ends = jnp.logical_and(frame < 2, band < reach)
    first_hop = jnp.logical_and(frame == FRAMES - 1, band >= reach)
    last_hop = jnp.logical_and(frame == 0, band >= reach)
    hops = jnp.logical_or(first_hop, last_hop)
    far_next = jnp.logical_and(frame == 0, band < reach)
    far_prev = jnp.logical_and(frame == 1, band < reach)
    greet = [(has[name], who[name]) for name in has]
    if detour:
        who["relay"] = lax.rem(idx + count - reach, count)
        who["end"] = lax.rem(idx + reach, count)
        who["over"] = jnp.where(
            first_hop, lax.rem(idx + 2 * reach, count), lax.rem(idx + count - 2 * reach, count))
        greet += [(ends, who["relay"]), (hops, who["end"]), (hops, who["over"])]

    def remote(src, dst, send, recv, name):
        return pltpu.make_async_remote_copy(
            src_ref=src, dst_ref=dst, send_sem=send, recv_sem=recv,
            device_id={"frames": who[name]}, device_id_type=MESH,
        )

    def start(copy, name):
        @pl.when(has[name])
        def _():
            copy.start()

    def landed(copy, name):
        @pl.when(has[name])
        def _():
            copy.wait_recv()

    sent = []

    loads = []
    for k in range(clips):
        loads.append(pltpu.make_async_copy(
            x_hbm.at[k], raw.at[k], x_sem.at[k]))
        loads[-1].start()
    weights = []
    for n, (src, dst) in enumerate(((in_hbm, win), (time_hbm, wtime), (mid_hbm, wmid), (up_hbm, wup))):
        weights.append(pltpu.make_async_copy(src, dst, w_sem.at[n]))
        weights[-1].start()

    barrier = pltpu.get_barrier_semaphore()
    for there, target in greet:
        @pl.when(there)
        def _(target=target):
            pl.semaphore_signal(
                barrier, inc=1, device_id={"frames": target}, device_id_type=MESH)
    pl.semaphore_wait(barrier, sum(there.astype(jnp.int32) for there, _ in greet))

    halo = {}
    for k in range(clips):
        for side, (to, row) in enumerate((("down", rows - 1), ("up", 0))):
            copy = remote(
                x_hbm.at[k, row], raw_got.at[k, side],
                h_send.at[k, side], h_recv.at[k, side], to)
            start(copy, to)
            halo[k, side] = copy
            sent.append((copy, to))
    sources = ("up", "down")
    steps = ("prev", "next")

    for side in range(2):
        @pl.when(jnp.logical_not(has[sources[side]]))
        def _(side=side):
            for k in range(clips):
                raw_got[k, side] = jnp.zeros((c, columns), BF16)
                edge_got[k, side] = jnp.zeros(edge_got.shape[2:], BF16)
        @pl.when(jnp.logical_not(has[steps[side]]))
        def _(side=side):
            for k in range(clips):
                got[k, side] = jnp.zeros(got.shape[2:], BF16)

    at = lax.broadcasted_iota(jnp.int32, (columns, columns), 0)
    to = lax.broadcasted_iota(jnp.int32, (columns, columns), 1)
    source = jnp.where(at < half, 2 * at, 2 * (at - half) + 1)
    split = jnp.where(to == source, 1.0, 0.0).astype(BF16)

    def place(k, slot, stored):
        value = lax.dot_general(
            split, stored, (((1,), (1,)), ((), ())), preferred_element_type=F32).astype(BF16)
        x3[k, slot, half:, :double] = jnp.concatenate([value[:half], value[half:]], axis=1)
        widen(x3, k, slot)

    def widen(dst, k, slot):
        row = dst[k, slot, half:, :double]
        even, odd = row[:, :c], row[:, c:]
        dst[k, slot, half:, double:] = sooner(even.astype(F32)).astype(BF16)
        dst[k, slot, :half, :] = jnp.concatenate(
            [later(odd.astype(F32)).astype(BF16), even, odd], axis=1)

    inner = list(range(1, rows - 1))
    order = inner + [0, rows - 1]
    parts = ((0, len(inner)), (len(inner), 2))

    def conv(src, k, picked, wref):
        total = None
        for dr in range(3):
            lhs = jnp.concatenate([src[k, r + dr] for r in picked], axis=0)
            term = mm(lhs, wref[dr].reshape(3 * c, c))
            total = term if total is None else total + term
        return total

    times = {}

    def first_part(k, part):
        at, size = parts[part]
        picked = order[at:at + size]
        value = silu(conv(x3, k, picked, win)).astype(BF16)
        for j in range(size):
            lo = 2 * half * j
            mine[k, at + j] = jnp.concatenate(
                [value[lo:lo + half], value[lo + half:lo + 2 * half]], axis=1)
        for side, to in ((0, "next"), (1, "prev")):
            copy = remote(
                mine.at[k, pl.ds(at, size)], got.at[k, side, pl.ds(at, size)],
                t_send.at[k, part, side], t_recv.at[k, part, side], to)
            if detour and part == 0:
                far = (far_next, far_prev)[side]
                by = remote(
                    mine.at[k, pl.ds(at, size)], passing.at[side, k],
                    t_send.at[k, part, side], r_recv.at[side, k], "relay")
                @pl.when(far)
                def _(by=by):
                    by.start()
                @pl.when(jnp.logical_and(has[to], jnp.logical_not(far)))
                def _(copy=copy):
                    copy.start()
            else:
                start(copy, to)
            times[k, part, side] = copy
            sent.append((copy, to))

    def over(flow, k):
        return remote(
            passing.at[flow, k], passing.at[flow, k],
            r_send.at[flow, k], r_recv.at[flow, k], "over")

    def home(flow, k):
        size = parts[0][1]
        return remote(
            passing.at[flow, k], got.at[k, flow, pl.ds(0, size)],
            r_send.at[flow, k], t_recv.at[k, 0, flow], "end")

    def pass_on(made, one, other):
        if not detour:
            return
        for k in range(clips):
            for there, flow in ((one, 0), (other, 1)):
                @pl.when(there)
                def _(flow=flow, k=k):
                    copy = made(flow, k)
                    over(flow, k).wait_recv()
                    copy.start()

    def stack(ref_value, size):
        v = ref_value.reshape(size * half, double)
        return jnp.concatenate([v[:, :c], v[:, c:]], axis=0)

    def own_part(k, part):
        at, size = parts[part]
        own = stack(mine[k, at:at + size], size)
        total = own.astype(F32) + mm(own, wtime[1])
        base[k, at:at + size] = total.reshape(size, columns, c)

    def skip_part(k, part):
        at, size = parts[part]
        total = base[k, at:at + size].reshape(size * columns, c)
        for side in range(2):
            landed(times[k, part, side], steps[side])
            total = total + mm(stack(got[k, side, at:at + size], size), wtime[2 * side])
        value = total.astype(BF16)
        n = size * half
        for j in range(size):
            s3[k, order[at + j] + 1, half:, :double] = jnp.concatenate(
                [value[j * half:(j + 1) * half], value[n + j * half:n + (j + 1) * half]], axis=1)

    edges = {}

    def share(k):
        pools = []
        for p in range(pooled_rows):
            pair = (s3[k, 2 * p + 1, half:, :double].astype(F32)
                    + s3[k, 2 * p + 2, half:, :double].astype(F32))
            pools.append(((pair[:, :c] + pair[:, c:]) * 0.25).astype(BF16))
        for side, (to, row, near) in enumerate((
            ("down", rows, pools[-2:]), ("up", 1, pools[:2]))):
            edge[k, side, 0] = s3[k, row, half:, :double]
            edge[k, side, 1] = jnp.concatenate(near, axis=1)
        for item in (1, 0):
            for side, to in enumerate(("down", "up")):
                copy = remote(
                    edge.at[k, side, item], edge_got.at[k, side, item],
                    e_send.at[k, side, item], e_recv.at[k, side, item], to)
                start(copy, to)
                edges[k, side, item] = copy
                sent.append((copy, to))
        for p in range(pooled_rows):
            spread(k, p + 2, pools[p])

    def spread(k, slot, pool):
        wide = pool.astype(F32)
        m3[k, slot] = jnp.concatenate(
            [later(wide).astype(BF16), pool, sooner(wide).astype(BF16)], axis=1)

    def turn_weights():
        for dr in range(3):
            turned = wup[dr].reshape(3 * c, -1).T
            wpool[dr] = turned[c:]
            for dw in range(3):
                wskip[dr, dw * c:(dw + 1) * c] = turned[:c, dw * c:(dw + 1) * c]

    def skip_weight(dr):
        return wskip[dr]

    wide = 2 * half

    def mid_weight(dr):
        return wmid[dr].reshape(3 * c, -1)

    def mid_inner(k):
        local = m3[k, 2:pooled_rows + 2].reshape(pooled_rows * half, 3 * c)
        mid_acc[k] = jnp.zeros(mid_acc.shape[1:], F32)
        for dr in range(3):
            term = mm(local, mid_weight(dr))
            mid_acc[k, 2 - dr:2 - dr + pooled_rows] += term.reshape(pooled_rows, half, -1)

    def up_inner(k):
        for r in range(rows):
            widen(s3, k, r + 1)
        centre = mm(s3[k, 1:rows + 1].reshape(rows * wide, 3 * c), skip_weight(1))
        acc[k] = centre.reshape(rows, wide, c)
        n = rows - 1
        lower = mm(s3[k, 1:rows].reshape(n * wide, 3 * c), skip_weight(0))
        acc[k, 1:rows] += lower.reshape(n, wide, c)
        upper = mm(s3[k, 2:rows + 1].reshape(n * wide, 3 * c), skip_weight(2))
        acc[k, :n] += upper.reshape(n, wide, c)

    def finish(k):
        for side in range(2):
            landed(edges[k, side, 1], sources[side])
            both = edge_got[k, side, 1]
            first_slot = (0, pooled_rows + 2)[side]
            spread(k, first_slot, both[:, :c])
            spread(k, first_slot + 1, both[:, c:])
        n = pooled_rows + 2
        mid_acc[k, :2] += mm(
            m3[k, :2].reshape(2 * half, 3 * c), mid_weight(0)).reshape(2, half, -1)
        mid_acc[k, n - 2:] += mm(
            m3[k, n:].reshape(2 * half, 3 * c), mid_weight(2)).reshape(2, half, -1)
        term = mm(jnp.concatenate([m3[k, 1], m3[k, n]], axis=0), mid_weight(1))
        mid_acc[k, 0] += term[:half]
        mid_acc[k, n - 1] += term[half:]
        total = mid_acc[k]
        value = silu(total).astype(BF16)
        middle[k] = value
        @pl.when(jnp.logical_not(has["up"]))
        def _():
            middle[k, 0] = jnp.zeros(middle.shape[2:], BF16)
        @pl.when(jnp.logical_not(has["down"]))
        def _():
            middle[k, n - 1] = jnp.zeros(middle.shape[2:], BF16)
        for side in range(2):
            landed(edges[k, side, 0], sources[side])
            slot = (0, rows + 1)[side]
            s3[k, slot, half:, :double] = edge_got[k, side, 0]
            widen(s3, k, slot)
        acc[k, 0] += mm(s3[k, 0], skip_weight(0))
        acc[k, rows - 1] += mm(s3[k, rows + 1], skip_weight(2))
        spans = ((0, n - 1), (1, n - 2), (1, n - 1))
        terms = {}
        for dr, (at, size) in enumerate(spans):
            lhs = middle[k, at:at + size].reshape(size * half, -1)
            term = mm(lhs, wpool[dr])
            for j in range(size):
                terms[dr, at + j] = term[j * half:(j + 1) * half]
        for r in range(rows):
            taps = sum(terms[dr, (r + dr + 1) // 2] for dr in range(3))
            cols = [taps[:, dw * c:(dw + 1) * c] for dw in range(3)]
            even = later(cols[0]) + cols[1] + cols[2] + acc[k, r, :half]
            odd = cols[0] + cols[1] + sooner(cols[2]) + acc[k, r, half:]
            own = x3[k, r + 1, half:, :double].astype(F32)
            value = jnp.concatenate([even + own[:, :c], odd + own[:, c:]], axis=0).astype(BF16)
            out_v[k, r] = mm(value.T, split).astype(BF16)
        copy = pltpu.make_async_copy(out_v.at[k], out_hbm.at[k], o_sem.at[k])
        copy.start()
        return copy

    weights[0].wait()
    for k in range(clips):
        loads[k].wait()
        for r in range(rows):
            place(k, r + 1, raw[k, r])
        first_part(k, 0)
    pass_on(over, first_hop, last_hop)
    for k in range(clips):
        for side in range(2):
            landed(halo[k, side], sources[side])
            place(k, (0, rows + 1)[side], raw_got[k, side])
        first_part(k, 1)
    for one in weights[1:]:
        one.wait()
    for k in range(clips):
        own_part(k, 0)
        own_part(k, 1)
    turn_weights()
    pass_on(home, last_hop, first_hop)
    outs = []
    for k in range(clips):
        skip_part(k, 0)
        skip_part(k, 1)
        share(k)
        if k > 0:
            outs.append(finish(k - 1))
        mid_inner(k)
        up_inner(k)
    outs.append(finish(clips - 1))
    for copy in outs:
        copy.wait()
    if detour:
        for flow in range(2):
            @pl.when(hops)
            def _(flow=flow):
                for k in range(clips):
                    over(flow, k).wait_send()
    for copy, to in sent:
        @pl.when(has[to])
        def _(copy=copy):
            copy.wait_send()


def body(count, latents, in_weight, time_weight, mid_weight, up_weight):
    clips, rows, columns, c = latents.shape
    cm = mid_weight.shape[-1]
    half, double = columns // 2, 2 * c
    flat = latents.swapaxes(2, 3)
    up_stored = up_weight.swapaxes(2, 3)
    dma = pltpu.SemaphoreType.DMA
    vmem = lambda *shape: pltpu.VMEM(shape, BF16)
    hbm = pl.BlockSpec(memory_space=pl.ANY)
    out = pl.pallas_call(
        functools.partial(kernel, count),
        out_shape=jax.ShapeDtypeStruct(flat.shape, BF16),
        in_specs=[hbm] * 5,
        out_specs=hbm,
        scratch_shapes=[
            vmem(clips, rows + 2, 2 * half, 3 * c),
            vmem(clips, rows + 2, 2 * half, 3 * c),
            vmem(clips, rows // 2 + 4, half, 3 * c),
            vmem(*in_weight.shape), vmem(*time_weight.shape),
            vmem(*mid_weight.shape), vmem(*up_stored.shape),
            vmem(3, 3 * c, c), vmem(3, cm, 3 * c),
            vmem(clips, rows, c, columns), vmem(clips, 2, c, columns),
            pltpu.VMEM((clips, rows, columns, c), F32),
            vmem(clips, rows, half, double),
            vmem(clips, 2, rows, half, double),
            vmem(clips, 2, 2, half, double),
            vmem(clips, 2, 2, half, double),
            vmem(clips, rows // 2 + 2, half, cm),
            pltpu.VMEM((clips, rows // 2 + 2, half, cm), F32),
            pltpu.VMEM((clips, rows, 2 * half, c), F32),
            vmem(clips, rows, c, columns), vmem(2, clips, rows - 2, half, double),
            dma((4,)), dma((clips,)), dma((clips,)),
            dma((clips, 2)), dma((clips, 2)),
            dma((clips, 2, 2)), dma((clips, 2, 2)),
            dma((clips, 2, 2)), dma((clips, 2, 2)),
            dma((2, clips)), dma((2, clips)),
        ],
        compiler_params=pltpu.CompilerParams(
            collective_id=0, has_side_effects=True, vmem_limit_bytes=60 * 1024 * 1024),
    )(flat, in_weight, time_weight, mid_weight, up_stored)
    return out.swapaxes(2, 3)


def solution(mesh):
    in_specs = (P("groups", "frames", None, None), P(), P(), P(), P())
    out_specs = P("groups", "frames", None, None)
    return jax.shard_map(
        functools.partial(body, mesh.shape["frames"]),
        mesh=mesh, in_specs=in_specs, out_specs=out_specs, check_vma=False)
```

profile of v0, /device:TPU:5, one launch (start us, length us, event | category | flops | bytes accessed | tf_op | source)
XLA Modules:
  0.0 42.6 jit_solution(1316598924414017059)
XLA Ops:
  0.0 40.7 %shard_map.55 = bf16[2,4,320,128]{3,2,1,0:T(8,128)(2,1)} custom-call(bf16[2,4,320,128]{3,2,1,0:T(8,128)(2,1)} %bitcast.5, bf16[3,3,320,320]{3,2,1,0:T(8,128)(2,1)} %in_hbm.1, bf16[3,320,320]{2,1,0:T(8,128)(2,1)} %time_hbm.1, bf16[3,3,320,640]{3,2,1,0:T(8,128)(2,1)} %mid_hbm.1, bf16[3,3,320,960]{3,2,1,0:T(8,128)(2,1)} %bitcast.3), custom_call_target="tpu_custom_call" | custom-call | tf_op jit(solution)/shard_map/pallas_call | solution.py:403
  40.7 2.0 %copy.7 = bf16[2,4,128,320]{2,3,1,0:T(8,128)(2,1)} copy(bf16[2,4,128,320]{2,3,1,0:T(8,128)(2,1)} %bitcast.4) | data formatting | bytes 1310720
where the time goes:
time: 42.8 us; the launch traced here: 42.6 us
  Pallas kernels  40.7 us (95%)
  local copies, waits for them, and re-layouts  1.97 us (5%)
    pallas_call x1, Pallas kernels, body(): pl.pallas_call(functools.partial(kernel, count), out_shape=jax.ShapeDtype...  40.7 us
    unnamed x1, local copies, waits for them, and re-layouts  1.97 us

commit v1 on v0

--- a/solution.py
+++ b/solution.py
@@ -343,10 +343,8 @@
             odd = cols[0] + cols[1] + sooner(cols[2]) + acc[k, r, half:]
             own = x3[k, r + 1, half:, :double].astype(F32)
             value = jnp.concatenate([even + own[:, :c], odd + own[:, c:]], axis=0).astype(BF16)
-            out_v[k, r] = mm(value.T, split).astype(BF16)
-        copy = pltpu.make_async_copy(out_v.at[k], out_hbm.at[k], o_sem.at[k])
-        copy.start()
-        return copy
+            out_hbm[k, r] = mm(value.T, split).astype(BF16)
+        return None
 
     weights[0].wait()
     for k in range(clips):
@@ -377,8 +375,6 @@
         mid_inner(k)
         up_inner(k)
     outs.append(finish(clips - 1))
-    for copy in outs:
-        copy.wait()
     if detour:
         for flow in range(2):
             @pl.when(hops)
@@ -402,9 +398,9 @@
     hbm = pl.BlockSpec(memory_space=pl.ANY)
     out = pl.pallas_call(
         functools.partial(kernel, count),
-        out_shape=jax.ShapeDtypeStruct(flat.shape, BF16),
+        out_shape=pltpu.VMEM(flat.shape, BF16),
         in_specs=[hbm] * 5,
-        out_specs=hbm,
+        out_specs=pl.BlockSpec(memory_space=pltpu.VMEM),
         scratch_shapes=[
             vmem(clips, rows + 2, 2 * half, 3 * c),
             vmem(clips, rows + 2, 2 * half, 3 * c),
@@ -429,8 +425,8 @@
             dma((2, clips)), dma((2, clips)),
         ],
         compiler_params=pltpu.CompilerParams(
-            collective_id=0, has_side_effects=True, vmem_limit_bytes=60 * 1024 * 1024),
-    )(flat, in_weight, time_weight, mid_weight, up_stored)
+            collective_id=0, has_side_effects=True, vmem_limit_bytes=50 * 1024 * 1024),
+    )(*[pltpu.with_memory_space_constraint(v, pltpu.HBM) for v in (flat, in_weight, time_weight, mid_weight, up_stored)])
     return out.swapaxes(2, 3)
 
 

time: 42.8 us -> 40.9 us (0.956)
  local copies, waits for them, and re-layouts: 1.97 us -> 0.84 us
  Pallas kernels: 40.7 us -> 39.9 us
    unnamed x1, local copies, waits for them, and re-layouts: 1.97 us -> 0.84 us
    pallas_call x1, Pallas kernels: 40.7 us -> 39.9 us  [body(): pl.pallas_call(functools.partial(kernel, count), out_shape=pltpu.VMEM(fla...]
where the time goes in v1:
time: 40.9 us; the launch traced here: 40.8 us
  Pallas kernels  39.9 us (98%)
  local copies, waits for them, and re-layouts  0.84 us (2%)
    pallas_call x1, Pallas kernels, body(): pl.pallas_call(functools.partial(kernel, count), out_shape=pltpu.VMEM(fla...  39.9 us
    unnamed x1, local copies, waits for them, and re-layouts  0.84 us

profile of v1, /device:TPU:5, one launch (start us, length us, event | category | flops | bytes accessed | tf_op | source)
XLA Modules:
  0.0 40.8 jit_solution(514682342782396434)
XLA Ops:
  0.0 39.9 %shard_map.55 = bf16[2,4,320,128]{3,2,1,0:T(8,128)(2,1)S(1)} custom-call(bf16[2,4,320,128]{3,2,1,0:T(8,128)(2,1)} %bitcast.5, bf16[3,3,320,320]{3,2,1,0:T(8,128)(2,1)} %in_hbm.1, bf16[3,320,320]{2,1,0:T(8,128)(2,1)} %time_hbm.1, bf16[3,3,320,640]{3,2,1,0:T(8,128)(2,1)} %mid_hbm.1, bf16[3,3,320,960]{3,2,1,0:T(8,128)(2,1)} %bitcast.4), custom_call_target="tpu_custom_call" | custom-call | tf_op jit(solution)/shard_map/pallas_call | solution.py:399
  39.9 0.8 %copy.7 = bf16[2,4,128,320]{2,3,1,0:T(8,128)(2,1)} copy(bf16[2,4,128,320]{2,3,1,0:T(8,128)(2,1)S(1)} %bitcast.3) | data formatting | bytes 1310720

commit v2 on v1

--- a/solution.py
+++ b/solution.py
@@ -173,7 +173,19 @@
             lo = 2 * half * j
             mine[k, at + j] = jnp.concatenate(
                 [value[lo:lo + half], value[lo + half:lo + 2 * half]], axis=1)
+
+    outer = jnp.logical_or(band == 0, band == bands - 1)
+    inside = jnp.logical_not(outer)
+
+    def send_part(k, part, now=None, way=None):
+        at, size = parts[part]
+        gate = lambda there: there if now is None else jnp.logical_and(there, now)
         for side, to in ((0, "next"), (1, "prev")):
+            if way is not None:
+                distant = (far_next, far_prev)[side]
+                mask = distant if way == "far" else jnp.logical_not(distant)
+                gate = lambda there, mask=mask: jnp.logical_and(
+                    there if now is None else jnp.logical_and(there, now), mask)
             copy = remote(
                 mine.at[k, pl.ds(at, size)], got.at[k, side, pl.ds(at, size)],
                 t_send.at[k, part, side], t_recv.at[k, part, side], to)
@@ -182,16 +194,19 @@
                 by = remote(
                     mine.at[k, pl.ds(at, size)], passing.at[side, k],
                     t_send.at[k, part, side], r_recv.at[side, k], "relay")
-                @pl.when(far)
+                @pl.when(gate(far))
                 def _(by=by):
                     by.start()
-                @pl.when(jnp.logical_and(has[to], jnp.logical_not(far)))
+                @pl.when(gate(jnp.logical_and(has[to], jnp.logical_not(far))))
                 def _(copy=copy):
                     copy.start()
             else:
-                start(copy, to)
-            times[k, part, side] = copy
-            sent.append((copy, to))
+                @pl.when(gate(has[to]))
+                def _(copy=copy):
+                    copy.start()
+            if (k, part, side) not in times:
+                times[k, part, side] = copy
+                sent.append((copy, to))
 
     def over(flow, k):
         return remote(
@@ -204,10 +219,10 @@
             passing.at[flow, k], got.at[k, flow, pl.ds(0, size)],
             r_send.at[flow, k], t_recv.at[k, 0, flow], "end")
 
-    def pass_on(made, one, other):
+    def pass_on(made, one, other, picked):
         if not detour:
             return
-        for k in range(clips):
+        for k in picked:
             for there, flow in ((one, 0), (other, 1)):
                 @pl.when(there)
                 def _(flow=flow, k=k):
@@ -287,16 +302,30 @@
             term = mm(local, mid_weight(dr))
             mid_acc[k, 2 - dr:2 - dr + pooled_rows] += term.reshape(pooled_rows, half, -1)
 
-    def up_inner(k):
-        for r in range(rows):
+    def up_first(k):
+        n = rows - 2
+        for r in range(1, rows - 1):
             widen(s3, k, r + 1)
-        centre = mm(s3[k, 1:rows + 1].reshape(rows * wide, 3 * c), skip_weight(1))
-        acc[k] = centre.reshape(rows, wide, c)
-        n = rows - 1
-        lower = mm(s3[k, 1:rows].reshape(n * wide, 3 * c), skip_weight(0))
-        acc[k, 1:rows] += lower.reshape(n, wide, c)
-        upper = mm(s3[k, 2:rows + 1].reshape(n * wide, 3 * c), skip_weight(2))
-        acc[k, :n] += upper.reshape(n, wide, c)
+        lhs = s3[k, 2:rows].reshape(n * wide, 3 * c)
+        acc[k, 1:rows - 1] = mm(lhs, skip_weight(1)).reshape(n, wide, c)
+        lower = mm(lhs, skip_weight(0)).reshape(n, wide, c)
+        acc[k, rows - 1] = lower[n - 1]
+        if n > 1:
+            acc[k, 2:rows - 1] += lower[:n - 1]
+        upper = mm(lhs, skip_weight(2)).reshape(n, wide, c)
+        acc[k, 0] = upper[0]
+        if n > 1:
+            acc[k, 1:rows - 2] += upper[1:]
+
+    def up_second(k):
+        for r in (0, rows - 1):
+            widen(s3, k, r + 1)
+        lhs = jnp.concatenate([s3[k, 1], s3[k, rows]], axis=0)
+        centre = mm(lhs, skip_weight(1))
+        acc[k, 0] += centre[:wide]
+        acc[k, rows - 1] += centre[wide:]
+        acc[k, 1] += mm(s3[k, 1], skip_weight(0))
+        acc[k, rows - 2] += mm(s3[k, rows], skip_weight(2))
 
     def finish(k):
         for side in range(2):
@@ -352,29 +381,43 @@
         for r in range(rows):
             place(k, r + 1, raw[k, r])
         first_part(k, 0)
-    pass_on(over, first_hop, last_hop)
+        send_part(k, 0, jnp.logical_not(hops) if detour and k > 0 else None)
+    pass_on(over, first_hop, last_hop, range(clips))
+    if detour:
+        for k in range(1, clips):
+            send_part(k, 0, hops)
     for k in range(clips):
         for side in range(2):
             landed(halo[k, side], sources[side])
             place(k, (0, rows + 1)[side], raw_got[k, side])
         first_part(k, 1)
+        if detour:
+            send_part(k, 1, None, "far")
+            if k == clips - 1:
+                for q in range(clips):
+                    send_part(q, 1, inside, "near")
+        else:
+            send_part(k, 1)
     for one in weights[1:]:
         one.wait()
     for k in range(clips):
         own_part(k, 0)
         own_part(k, 1)
     turn_weights()
-    pass_on(home, last_hop, first_hop)
-    outs = []
+    pass_on(home, last_hop, first_hop, range(clips))
+    for k in range(clips):
+        if detour:
+            send_part(k, 1, outer, "near")
     for k in range(clips):
         skip_part(k, 0)
+        up_first(k)
         skip_part(k, 1)
         share(k)
         if k > 0:
-            outs.append(finish(k - 1))
+            finish(k - 1)
         mid_inner(k)
-        up_inner(k)
-    outs.append(finish(clips - 1))
+        up_second(k)
+    finish(clips - 1)
     if detour:
         for flow in range(2):
             @pl.when(hops)

time: 40.9 us -> 40.5 us (level)
  Pallas kernels: 39.9 us -> 39.4 us
    pallas_call x1, Pallas kernels: 39.9 us -> 39.4 us  [body(): pl.pallas_call(functools.partial(kernel, count), out_shape=pltpu.VMEM(fla...]
where the time goes in v2:
time: 40.5 us; the launch traced here: 40.2 us
  Pallas kernels  39.4 us (97%)
  local copies, waits for them, and re-layouts  0.84 us (2%)
    pallas_call x1, Pallas kernels, body(): pl.pallas_call(functools.partial(kernel, count), out_shape=pltpu.VMEM(fla...  39.4 us
    unnamed x1, local copies, waits for them, and re-layouts  0.84 us

profile of v2, /device:TPU:5, one launch (start us, length us, event | category | flops | bytes accessed | tf_op | source)
XLA Modules:
  0.0 40.2 jit_solution(12488276276062764914)
XLA Ops:
  0.0 39.4 %shard_map.55 = bf16[2,4,320,128]{3,2,1,0:T(8,128)(2,1)S(1)} custom-call(bf16[2,4,320,128]{3,2,1,0:T(8,128)(2,1)} %bitcast.5, bf16[3,3,320,320]{3,2,1,0:T(8,128)(2,1)} %in_hbm.1, bf16[3,320,320]{2,1,0:T(8,128)(2,1)} %time_hbm.1, bf16[3,3,320,640]{3,2,1,0:T(8,128)(2,1)} %mid_hbm.1, bf16[3,3,320,960]{3,2,1,0:T(8,128)(2,1)} %bitcast.4), custom_call_target="tpu_custom_call" | custom-call | tf_op jit(solution)/shard_map/pallas_call | solution.py:442
  39.4 0.8 %copy.7 = bf16[2,4,128,320]{2,3,1,0:T(8,128)(2,1)} copy(bf16[2,4,128,320]{2,3,1,0:T(8,128)(2,1)S(1)} %bitcast.3) | data formatting | bytes 1310720

commit v3 on v2

--- a/solution.py
+++ b/solution.py
@@ -381,16 +381,17 @@
         for r in range(rows):
             place(k, r + 1, raw[k, r])
         first_part(k, 0)
-        send_part(k, 0, jnp.logical_not(hops) if detour and k > 0 else None)
-    pass_on(over, first_hop, last_hop, range(clips))
-    if detour:
-        for k in range(1, clips):
-            send_part(k, 0, hops)
+        send_part(k, 0, jnp.logical_not(jnp.logical_and(hops, outer)) if detour and k > 0 else None)
+    pass_on(over, first_hop, last_hop, [0])
     for k in range(clips):
         for side in range(2):
             landed(halo[k, side], sources[side])
             place(k, (0, rows + 1)[side], raw_got[k, side])
         first_part(k, 1)
+        if k == 0 and detour:
+            pass_on(over, first_hop, last_hop, range(1, clips))
+            for q in range(1, clips):
+                send_part(q, 0, jnp.logical_and(hops, outer))
         if detour:
             send_part(k, 1, None, "far")
             if k == clips - 1:

time: 40.5 us -> 39.9 us (0.985)
  the two profiles are of different devices: /device:TPU:5 before, /device:TPU:11 now
where the time goes in v3:
time: 39.9 us; the launch traced here: 39.8 us
  Pallas kernels  38.9 us (97%)
  local copies, waits for them, and re-layouts  0.84 us (2%)
    pallas_call x1, Pallas kernels, body(): pl.pallas_call(functools.partial(kernel, count), out_shape=pltpu.VMEM(fla...  38.9 us
    unnamed x1, local copies, waits for them, and re-layouts  0.84 us

profile of v3, /device:TPU:11, one launch (start us, length us, event | category | flops | bytes accessed | tf_op | source)
XLA Modules:
  0.0 39.8 jit_solution(17290122001938411234)
XLA Ops:
  0.0 38.9 %shard_map.55 = bf16[2,4,320,128]{3,2,1,0:T(8,128)(2,1)S(1)} custom-call(bf16[2,4,320,128]{3,2,1,0:T(8,128)(2,1)} %bitcast.5, bf16[3,3,320,320]{3,2,1,0:T(8,128)(2,1)} %in_hbm.1, bf16[3,320,320]{2,1,0:T(8,128)(2,1)} %time_hbm.1, bf16[3,3,320,640]{3,2,1,0:T(8,128)(2,1)} %mid_hbm.1, bf16[3,3,320,960]{3,2,1,0:T(8,128)(2,1)} %bitcast.4), custom_call_target="tpu_custom_call" | custom-call | tf_op jit(solution)/shard_map/pallas_call | solution.py:443
  38.9 0.8 %copy.7 = bf16[2,4,128,320]{2,3,1,0:T(8,128)(2,1)} copy(bf16[2,4,128,320]{2,3,1,0:T(8,128)(2,1)S(1)} %bitcast.3) | data formatting | bytes 1310720

commit v4 on v3

--- a/solution.py
+++ b/solution.py
@@ -381,7 +381,7 @@
         for r in range(rows):
             place(k, r + 1, raw[k, r])
         first_part(k, 0)
-        send_part(k, 0, jnp.logical_not(jnp.logical_and(hops, outer)) if detour and k > 0 else None)
+        send_part(k, 0)
     pass_on(over, first_hop, last_hop, [0])
     for k in range(clips):
         for side in range(2):
@@ -390,8 +390,6 @@
         first_part(k, 1)
         if k == 0 and detour:
             pass_on(over, first_hop, last_hop, range(1, clips))
-            for q in range(1, clips):
-                send_part(q, 0, jnp.logical_and(hops, outer))
         if detour:
             send_part(k, 1, None, "far")
             if k == clips - 1:

time: 39.9 us -> 40 us (level)
  no operation moved by 1% of the time
where the time goes in v4:
time: 40 us; the launch traced here: 39.9 us
  Pallas kernels  39 us (98%)
  local copies, waits for them, and re-layouts  0.84 us (2%)
    pallas_call x1, Pallas kernels, body(): pl.pallas_call(functools.partial(kernel, count), out_shape=pltpu.VMEM(fla...  39 us
    unnamed x1, local copies, waits for them, and re-layouts  0.84 us

profile of v4, /device:TPU:11, one launch (start us, length us, event | category | flops | bytes accessed | tf_op | source)
XLA Modules:
  0.0 39.9 jit_solution(9719811891391696373)
XLA Ops:
  0.0 39.0 %shard_map.55 = bf16[2,4,320,128]{3,2,1,0:T(8,128)(2,1)S(1)} custom-call(bf16[2,4,320,128]{3,2,1,0:T(8,128)(2,1)} %bitcast.5, bf16[3,3,320,320]{3,2,1,0:T(8,128)(2,1)} %in_hbm.1, bf16[3,320,320]{2,1,0:T(8,128)(2,1)} %time_hbm.1, bf16[3,3,320,640]{3,2,1,0:T(8,128)(2,1)} %mid_hbm.1, bf16[3,3,320,960]{3,2,1,0:T(8,128)(2,1)} %bitcast.4), custom_call_target="tpu_custom_call" | custom-call | tf_op jit(solution)/shard_map/pallas_call | solution.py:441
  39.0 0.8 %copy.7 = bf16[2,4,128,320]{2,3,1,0:T(8,128)(2,1)} copy(bf16[2,4,128,320]{2,3,1,0:T(8,128)(2,1)S(1)} %bitcast.3) | data formatting | bytes 1310720
